TPU v7x, 32 devices: a whole 2x2x4 slice. The times are simulated.
32 devices in a mesh: layer: 4 (over y, core), feat: 4 (over z), path: 2 (over x).
Axes of the slice: x: 2, y: 2, z: 4, core: 2. Of those that a mesh axis runs over, the one named last changes fastest.
Arguments:
- context: bfloat16 [4, 64, 2304], P('layer'), may hold values from -6 to 6
- targets: bfloat16 [4, 64, 2304], P('layer'), may hold values from -4 to 4
- beyond_targets: bfloat16 [64, 2304], replicated, may hold values from -4 to 4
- positions: int32 [32], replicated, may hold values from 0 to 63
- donors: int32 [32], replicated, may hold values from 0 to 63
- encoder: bfloat16 [4, 2304, 8192], P('layer', None, 'feat'), may hold values from -0.125 to 0.125
- encoder_bias: float32 [4, 8192], P('layer', 'feat'), may hold values from -3 to 3
- decoder: bfloat16 [4, 2, 8192, 2304], P('layer', None, 'feat', 'path'), may hold values from -0.0625 to 0.0625
Outputs:
- attribution: float32 [4, 32, 2304], P('layer', None, ('feat', 'path'))
All inputs are finite; a program needn't handle non-finite values.
Results may differ from a plain program's by a relative error of at most 0.0071.
Values may be sent and summed in bfloat16 or wider, within the bound.
A program may use at most 64 MiB of HBM per device.

v0:
```python
import jax
import jax.numpy as jnp
from jax import lax
from jax.sharding import PartitionSpec as P

PTS_DEV = 4


def from_behind(block, axis, distance):
    devices = range(lax.axis_size(axis))
    route = [(i - distance, i) for i in devices if i - distance in devices]
    return lax.ppermute(block, axis, route)


def decode_errors(parts, goal_rows, goal_next, layer_here, last_layer):
    own, later = lax.psum((parts[0], parts[1]), "feat")
    incoming = from_behind(later, "layer", 1)
    height = goal_rows.shape[0]
    columns = own.shape[1]
    rebuilt = (own + incoming).reshape(-1, height, columns)
    errors_here = (rebuilt - goal_rows[None]).astype(jnp.bfloat16).reshape(-1, columns)
    errors_last = (
        (later.reshape(-1, height, columns) - goal_next[None])
        .astype(jnp.bfloat16)
        .reshape(-1, columns)
    )
    from_next = from_behind(errors_here, "layer", -1)
    errors_next = jnp.where(layer_here == last_layer, errors_last, from_next)
    stacked = jnp.stack([errors_here, errors_next])
    return stacked


def per_device(context, targets, beyond_targets, positions, donors, encoder, encoder_bias, decoder):
    layer_here = lax.axis_index("layer")
    last_layer = lax.axis_size("layer") - 1
    path_count = lax.axis_size("path")
    feat_count = lax.axis_size("feat")
    path_here = lax.axis_index("path")
    model_width = context.shape[2]
    height = positions.shape[0]
    points = PTS_DEV * path_count
    point_index = path_here * PTS_DEV + jnp.arange(PTS_DEV, dtype=jnp.int32)
    fraction = (point_index.astype(jnp.float32) + 0.5) / points
    source_rows = context[0][positions].astype(jnp.float32)
    donor_rows = context[0][donors].astype(jnp.float32)
    offset = source_rows - donor_rows
    inputs = (
        (donor_rows[None] + fraction[:, None, None] * offset[None])
        .astype(jnp.bfloat16)
        .reshape(-1, model_width)
    )
    preact = jnp.dot(inputs, encoder[0], preferred_element_type=jnp.float32) + encoder_bias[0]
    code_rows = jnp.maximum(preact, 0.0).astype(jnp.bfloat16)
    goal_rows = targets[0][positions].astype(jnp.float32)
    goal_next = beyond_targets[positions].astype(jnp.float32)
    columns = model_width // path_count
    gathered = lax.all_gather(code_rows, "path", axis=0, tiled=True)
    parts = jnp.einsum("rf,jfd->jrd", gathered, decoder[0], preferred_element_type=jnp.float32)
    goal_cols = lax.dynamic_slice_in_dim(goal_rows, path_here * columns, columns, 1)
    next_cols = lax.dynamic_slice_in_dim(goal_next, path_here * columns, columns, 1)
    errors = decode_errors(parts, goal_cols, next_cols, layer_here, last_layer)
    partial_grads = jnp.einsum(
        "jrd,jfd->rf", errors, decoder[0], preferred_element_type=jnp.float32
    )
    grads = lax.psum_scatter(partial_grads, "path", scatter_dimension=0, tiled=True)
    gated = jnp.where(preact > 0, grads, 0.0).astype(jnp.bfloat16)
    input_grads = jnp.einsum("rf,df->rd", gated, encoder[0], preferred_element_type=jnp.float32)
    summed = input_grads.reshape(-1, height, model_width).sum(axis=0)
    quadrature = lax.psum_scatter(summed, ("feat", "path"), scatter_dimension=1, tiled=True)
    block_cols = model_width // (feat_count * path_count)
    block_index = lax.axis_index("feat") * path_count + path_here
    offset_cols = lax.dynamic_slice_in_dim(offset, block_index * block_cols, block_cols, 1)
    return (offset_cols * quadrature / points)[None]


def solution(mesh):
    placed = (
        P("layer", None, None),
        P("layer", None, None),
        P(),
        P(),
        P(),
        P("layer", None, "feat"),
        P("layer", "feat"),
        P("layer", None, "feat", "path"),
    )
    return jax.shard_map(
        per_device,
        mesh=mesh,
        in_specs=placed,
        out_specs=P("layer", None, ("feat", "path")),
        check_vma=False,
    )
```

profile of v0, /device:TPU:1, one launch (start us, length us, event | category | flops | bytes accessed | tf_op | source)
XLA Modules:
  0.0 293.9 jit_solution(9656341304683509730)
XLA Ops:
  6.5 0.7 compare_select_fusion
  7.3 0.3 copy-done
  7.5 0.7 gather_fusion
  8.2 0.7 gather_fusion.1
  8.9 0.2 add_convert_fusion
  9.1 0.4 copy-done.5
  9.5 6.0 %maximum_convert_fusion = (bf16[128,2048]{1,0:T(8,128)(2,1)}, f32[128,2048]{1,0:T(8,128)S(1)}) fusion(f32[2048]{0:T(1024)S(1)} %bitcast.63, bf16[128,2304]{1,0:T(8,128)(2,1)S(1)} %bitcast.59, bf16[1,2304,2048]{2,1,0:T(8,128)(2,1)} %param.13), kind=kOutput, calls=%fused_computation.28 | convolution fusion | flops 1208745984 | bytes 11608064 | tf_op jit(solution)/shard_map/dot_general | solution.py:52
  15.5 0.0 all-gather.2.cloned.1.call-update
  15.6 0.0 all-reduce.3.cloned.1.call-start
  15.6 23.3 %all-gather.2.cloned.1.call-done = bf16[256,2048]{1,0:T(8,128)(2,1)} async-done(((bf16[128,2048]{1,0:T(8,128)(2,1)}), bf16[256,2048]{1,0:T(8,128)(2,1)}) %all-gather.2.cloned.1.call-update) | async-done | bytes 1048592 | tf_op jit(solution)/shard_map/all_gather | solution.py:57
  38.9 6.6 %fusion.8 = f32[2,256,1152]{2,1,0:T(8,128)S(1)} fusion(bf16[1,2,2048,1152]{3,2,1,0:T(8,128)(2,1)} %param.15, bf16[256,2048]{1,0:T(8,128)(2,1)} %all-gather.2.cloned.1.call-done), kind=kOutput, calls=%fused_computation.12 | convolution fusion | flops 2415919104 | bytes 12845056 | tf_op jit(solution)/shard_map/rf,jfd->jrd/dot_general | solution.py:58
  45.5 1.6 slice_bitcast_fusion
  47.1 0.0 all-reduce.3.cloned.1.call-update
  47.1 0.0 reduce-scatter.5.cloned.1.call-start
  47.1 94.8 %all-reduce.3.cloned.1.call-done = (f32[256,1152]{1,0:T(8,128)}, f32[256,1152]{1,0:T(8,128)}) async-done(((f32[256,1152]{1,0:T(8,128)}, f32[256,1152]{1,0:T(8,128)}), (f32[256,1152]{1,0:T(8,128)}, f32[256,1152]{1,0:T(8,128)})) %all-reduce.3.cloned.1.call-update) | async-done | bytes 2359312 | tf_op jit(solution)/shard_map/psum | solution.py:16
  141.9 3.9 %collective-permute-start = (f32[256,1152]{1,0:T(8,128)}, f32[256,1152]{1,0:T(8,128)}, u32[]{:S(2)}, u32[]{:S(2)}) collective-permute-start(f32[256,1152]{1,0:T(8,128)} %get-tuple-element.6), channel_id=1, source_target_pairs={{0,8},{8,16},{16,24},{1,9},{9,17},{17,25},{2,10},{10,18},{18,26},{... | collective-permute-start | bytes 3538952 | tf_op jit(solution)/shard_map/ppermute | solution.py:12
  145.9 0.7 gather_fusion.2
  146.6 12.7 %collective-permute-done = f32[256,1152]{1,0:T(8,128)} collective-permute-done((f32[256,1152]{1,0:T(8,128)}, f32[256,1152]{1,0:T(8,128)}, u32[]{:S(2)}, u32[]{:S(2)}) %collective-permute-start) | collective-permute-done | bytes 1179680 | tf_op jit(solution)/shard_map/ppermute | solution.py:12
  159.3 2.3 fusion.24
  161.6 2.0 collective-permute-start.1
  163.6 0.7 gather_fusion.3
  164.3 9.6 %collective-permute-done.1 = bf16[256,1152]{1,0:T(8,128)(2,1)} collective-permute-done((bf16[256,1152]{1,0:T(8,128)(2,1)}, bf16[256,1152]{1,0:T(8,128)(2,1)}, u32[]{:S(2)}, u32[]{:S(2)}) %collective-permute-start.1) | collective-permute-done | bytes 589856 | tf_op jit(solution)/shard_map/ppermute | solution.py:12
  174.0 1.2 fusion.26
  175.2 7.8 %fusion.11 = f32[256,2048]{1,0:T(8,128)} fusion(bf16[1,2,2048,1152]{3,2,1,0:T(8,128)(2,1)} %param.15, bf16[1,256,1152]{2,1,0:T(8,128)(2,1)S(1)} %bitcast.61, bf16[1,256,1152]{2,1,0:T(8,128)(2,1)} %bitcast.11), kind=kOutput, calls=%fused_computation.13 | convolution fusion | flops 2416508928 | bytes 12713984 | tf_op jit(solution)/shard_map/jrd,jfd->rf/dot_general | solution.py:62
  183.1 0.0 reduce-scatter.7.cloned.1.call-start
  183.1 29.5 %reduce-scatter.5.cloned.1.call-done = f32[128,2048]{1,0:T(8,128)} async-done(((f32[256,2048]{1,0:T(8,128)}), f32[128,2048]{1,0:T(8,128)}) %reduce-scatter.5.cloned.1.call-update) | async-done | bytes 1048592 | tf_op jit(solution)/shard_map/reduce_scatter | solution.py:65
  212.6 1.3 select_convert_fusion
  213.9 6.9 %fusion.17 = f32[32,2304]{1,0:T(8,128)S(1)} fusion(bf16[4,32,2048]{2,1,0:T(8,128)(2,1)S(1)} %bitcast.60, bf16[1,2304,2048]{2,1,0:T(8,128)(2,1)} %param.13), kind=kOutput, calls=%fused_computation.15 | convolution fusion | flops 1208180736 | bytes 10256384 | tf_op jit(solution)/shard_map/rf,df->rd/dot_general | solution.py:67
  220.9 1.4 copy.9
  222.3 63.3 %reduce-scatter.7.cloned.1.call-done = f32[288,32]{1,0:T(8,128)} async-done(((f32[2304,32]{1,0:T(8,128)}), f32[288,32]{1,0:T(8,128)}) %reduce-scatter.7.cloned.1.call-update) | async-done | bytes 36880
  285.6 1.0 copy.10
  286.6 0.7 multiply_bitcast_fusion
  (20 shorter events, 0.2 us)
Async XLA Ops:
  6.5 1.0 copy-start
  6.5 32.4 %all-gather.2.cloned.1.call-start = ((), (), s32[]{:S(2)}) async-start(), calls=%async_computation.2 | async-start | bytes 1572864 | tf_op jit(solution)/shard_map/all_gather | solution.py:57
  8.8 0.7 copy-start.5
  15.6 126.4 %all-reduce.3.cloned.1.call-start = ((), (), s32[]{:S(2)}) async-start(), calls=%async_computation.5 | async-start | bytes 4718592 | tf_op jit(solution)/shard_map/psum | solution.py:16
  47.1 98.8 %copy-start.1 = (bf16[1,64,2304]{2,1,0:T(8,128)(2,1)S(1)}, bf16[1,64,2304]{2,1,0:T(8,128)(2,1)}, u32[]{:S(2)}) copy-start(bf16[1,64,2304]{2,1,0:T(8,128)(2,1)} %param.9) | copy-start | bytes 884740
  47.1 165.5 %reduce-scatter.5.cloned.1.call-start = ((), (), s32[]{:S(2)}) async-start(), calls=%async_computation.3 | async-start | bytes 3145728 | tf_op jit(solution)/shard_map/reduce_scatter | solution.py:65
  141.9 17.4 %copy-start.3 = (f32[256,1152]{1,0:T(8,128)S(1)}, f32[256,1152]{1,0:T(8,128)}, u32[]{:S(2)}) copy-start(f32[256,1152]{1,0:T(8,128)} %get-tuple-element.5) | copy-start | bytes 3538948
  141.9 17.4 %collective-permute-start = (f32[256,1152]{1,0:T(8,128)}, f32[256,1152]{1,0:T(8,128)}, u32[]{:S(2)}, u32[]{:S(2)}) collective-permute-start(f32[256,1152]{1,0:T(8,128)} %get-tuple-element.6), channel_id=1, source_target_pairs={{0,8},{8,16},{16,24},{1,9},{9,17},{17,25},{2,10},{10,18},{18,26},{... | collective-permute-start | bytes 3538952 | tf_op jit(solution)/shard_map/ppermute | solution.py:12
  159.3 4.3 %copy-start.2 = (bf16[64,2304]{1,0:T(8,128)(2,1)S(1)}, bf16[64,2304]{1,0:T(8,128)(2,1)}, u32[]{:S(2)}) copy-start(bf16[64,2304]{1,0:T(8,128)(2,1)} %param.10) | copy-start | bytes 884740
  161.6 12.4 %copy-start.4 = (f32[256,1152]{1,0:T(8,128)S(1)}, f32[256,1152]{1,0:T(8,128)}, u32[]{:S(2)}) copy-start(f32[256,1152]{1,0:T(8,128)} %get-tuple-element.6) | copy-start | bytes 3538948
  161.6 12.4 %collective-permute-start.1 = (bf16[256,1152]{1,0:T(8,128)(2,1)}, bf16[256,1152]{1,0:T(8,128)(2,1)}, u32[]{:S(2)}, u32[]{:S(2)}) collective-permute-start(bf16[256,1152]{1,0:T(8,128)(2,1)} %fusion.24), channel_id=1, source_target_pairs={{8,0},{16,8},{24,16},{9,1},{17,9},{25,17},{10,2},{18,10},{26,18},{... | collective-permute-start | bytes 1769480 | tf_op jit(solution)/shard_map/ppermute | solution.py:12
  183.1 102.5 %reduce-scatter.7.cloned.1.call-start = ((), (), s32[]{:S(2)}) async-start(), calls=%async_computation.4 | async-start | bytes 1327104
Sparse Core Ops, SparseCore 0:
  15.7 23.1 all-gather.1
  47.2 94.6 all-reduce.2
  183.2 29.3 reduce-scatter.4
  222.4 63.1 reduce-scatter.6
where the time goes:
time: 297 us; the launch traced here: 294 us
  waiting for transfers between devices  233 us (78%)
  matrix products  27.3 us (9%)
  between operations  13.3 us (4%)
  local copies, waits for them, and re-layouts  7.28 us (2%)
  other arithmetic  6.58 us (2%)
  starting transfers between devices  6.12 us (2%)
    psum x1, waiting for transfers between devices, decode_errors(): own, later = lax.psum((parts[0], parts[1]), 'feat')  94.8 us
    unnamed x5, waiting for transfers between devices  63.4 us
    reduce_scatter x1, waiting for transfers between devices, per_device(): lax.psum_scatter(partial_grads, 'path', scatter_dimension=0, tiled=True)  29.5 us
    all_gather x1, waiting for transfers between devices, per_device(): gathered = lax.all_gather(code_rows, 'path', axis=0, tiled=True)  23.3 us
    ppermute x2, waiting for transfers between devices, from_behind(): return lax.ppermute(block, axis, route)  22.4 us
    dot_general x1, matrix products, per_device(): jnp.einsum('jrd,jfd->rf', errors, decoder[0], preferred_element_type=jnp....  7.84 us
    dot_general x1, matrix products, per_device(): jnp.einsum('rf,df->rd', gated, encoder[0], preferred_element_type=jnp.flo...  6.91 us
    dot_general x1, matrix products, per_device(): jnp.einsum('rf,jfd->jrd', gathered, decoder[0], preferred_element_type=jn...  6.61 us
  transfers between devices with their start and end apart: 6, of which 6 were waited for; matrix products, arithmetic and copies ran while one was open for 0% of the time, Pallas kernels for 0%

commit v1 on v0

v1 whole, which is shorter than its diff:
```python
import functools

import jax
import jax.numpy as jnp
from jax import lax
from jax.experimental import pallas as pl
from jax.experimental.pallas import tpu as pltpu
from jax.sharding import PartitionSpec as P

PTS_DEV = 4
CHUNKS = 8
MESH = pl.DeviceIdType.MESH
NT = (((1,), (1,)), ((), ()))


def tile_of(width, most):
    sizes = [t for t in range(128, most + 1, 128) if width % t == 0]
    return sizes[-1] if sizes else width


def aligned(start, size):
    return pl.ds(pl.multiple_of(start, size), size)


def kernel(
    shape, pos_ref, don_ref, ctx_ref, tgt_ref, bey_ref, bias_ref, ctxb_ref, enc_hbm, dec_hbm, out_ref,
    enc, dec, inputs, codes, own, later, later_in, goal, red_recv, red_send, err, gsum, part, final_send, final_recv,
    enc_sem, dec_sem, later_sem, red_sem, err_sem, next_sem, final_sem,
):
    layers, n, paths = shape
    layer, z, path = lax.axis_index("layer"), lax.axis_index("feat"), lax.axis_index("path")
    last = layers - 1
    height, tokens = pos_ref.shape[0], ctx_ref.shape[0]
    rows, width = inputs.shape
    feats, cols = codes.shape[1], own.shape[1]
    points = rows // height
    half = rows // 2
    chunk = half // CHUNKS
    groups = n * paths
    me = z * paths + path
    scatter = final_send is not None

    barrier = pltpu.get_barrier_semaphore()

    def greet(i, carry):
        other = lax.rem(me + 1 + i, groups)
        pl.semaphore_signal(
            barrier, inc=1, device_id={"feat": other // paths, "path": lax.rem(other, paths)}, device_id_type=MESH
        )
        return carry

    lax.fori_loop(0, groups - 1, greet, 0)

    @pl.when(layer > 0)
    def _():
        pl.semaphore_signal(barrier, inc=1, device_id={"layer": layer - 1}, device_id_type=MESH)

    @pl.when(layer < last)
    def _():
        pl.semaphore_signal(barrier, inc=1, device_id={"layer": layer + 1}, device_id_type=MESH)

    ftile = tile_of(feats, 256)
    ftiles = feats // ftile

    def enc_copy(j):
        return pltpu.make_async_copy(
            enc_hbm.at[0, :, aligned(j * ftile, ftile)], enc.at[:, aligned(j * ftile, ftile)], enc_sem.at[j]
        )

    def dec_copy(k):
        return pltpu.make_async_copy(dec_hbm.at[0, k], dec.at[k], dec_sem.at[k])

    for j in range(ftiles):
        enc_copy(j).start()
    dec_copy(1).start()
    dec_copy(0).start()

    token = lax.broadcasted_iota(jnp.int32, (height, tokens), 1)
    pick_source = (token == pos_ref[...]).astype(jnp.float32).astype(jnp.bfloat16)
    pick_donor = (token == don_ref[...]).astype(jnp.float32).astype(jnp.bfloat16)

    def pick(which, ref):
        return jnp.dot(which, ref[...], preferred_element_type=jnp.float32)

    donor = pick(pick_donor, ctx_ref)
    offset = pick(pick_source, ctx_ref) - donor
    for p in range(points):
        inputs[p * height : (p + 1) * height, :] = (donor + ((p + 0.5) / points) * offset).astype(jnp.bfloat16)
    goals = (pick(pick_source, tgt_ref).astype(jnp.bfloat16), pick(pick_source, bey_ref).astype(jnp.bfloat16))
    for p in range(points):
        for k in (0, 1):
            goal[k, p * height : (p + 1) * height, :] = goals[k]

    @pl.when(layer == 0)
    def _():
        later_in[...] = jnp.zeros_like(later_in)

    def encode(j, carry):
        enc_copy(j).wait()
        at = aligned(j * ftile, ftile)
        preact = jnp.dot(inputs[...], enc[:, at], preferred_element_type=jnp.float32) + bias_ref[:, at]
        codes[:, at] = jnp.maximum(preact, 0.0).astype(jnp.bfloat16)
        return carry

    lax.fori_loop(0, ftiles, encode, 0)

    ctile = tile_of(cols, 384)

    def decode(k, into):
        def step(j, carry):
            at = aligned(j * ctile, ctile) if cols > ctile else slice(None)
            value = jnp.dot(codes[...], dec[k, :, at], preferred_element_type=jnp.float32)
            into[:, at] = value.astype(into.dtype)
            return carry

        dec_copy(k).wait()
        lax.fori_loop(0, cols // ctile, step, 0)

    decode(1, later)

    pl.semaphore_wait(barrier, groups - 1 + jnp.minimum(layer, 1) + jnp.minimum(last - layer, 1))

    def at_rows(d, c):
        return aligned(d * half + c * chunk, chunk)

    def later_copy(d, c):
        at = at_rows(d, c)
        return pltpu.make_async_remote_copy(
            later.at[at, :], later_in.at[at, :], later_sem.at[0, d, c], later_sem.at[1, d, c],
            device_id={"layer": lax.rem(layer + 1, layers)}, device_id_type=MESH,
        )

    def place(d):
        return (n - 1 - z, z - 1, z + 1) if d == 0 else (z, z + 1, z - 1)

    def wrap(i):
        return lax.rem(i + n, n)

    def red_copy(k, d, c):
        at = at_rows(d, c)
        return pltpu.make_async_remote_copy(
            red_send.at[k, at, :], red_recv.at[k, at, :], red_sem.at[0, k, d, c], red_sem.at[1, k, d, c],
            device_id={"feat": wrap(place(d)[1])}, device_id_type=MESH,
        )

    def err_copy(k, d, c):
        at = at_rows(d, c)
        return pltpu.make_async_remote_copy(
            err.at[k, at, :], err.at[k, at, :], err_sem.at[0, k, d, c], err_sem.at[1, k, d, c],
            device_id={"feat": wrap(place(d)[2])}, device_id_type=MESH,
        )

    def next_copy(d, c):
        at = at_rows(d, c)
        return pltpu.make_async_remote_copy(
            err.at[0, at, :], err.at[1, at, :], next_sem.at[0, d, c], next_sem.at[1, d, c],
            device_id={"layer": lax.rem(layer + last, layers)}, device_id_type=MESH,
        )

    def each_chunk(act):
        def step(c, carry):
            for d in (0, 1):
                act(d, c)
            return carry

        lax.fori_loop(0, CHUNKS, step, 0)

    @pl.when(layer < last)
    def _():
        each_chunk(lambda d, c: later_copy(d, c).start())

    decode(0, own)

    def hand_on(k, d, c):
        @pl.when(place(d)[0] > 0)
        def _():
            err_copy(k, d, c).start()

        if k == 0:

            @pl.when(layer > 0)
            def _():
                next_copy(d, c).start()

    def reduce_step(k, d, c):
        at = at_rows(d, c)
        position = place(d)[0]

        def base():
            if k == 1:
                return later[at, :].astype(jnp.float32)
            return own[at, :] + later_in[at, :].astype(jnp.float32)

        if k == 0:

            @pl.when(layer > 0)
            def _():
                later_copy(d, c).wait_recv()

        @pl.when(position == 0)
        def _():
            red_send[k, at, :] = base().astype(jnp.bfloat16)
            red_copy(k, d, c).start()

        @pl.when(position > 0)
        def _():
            red_copy(k, d, c).wait_recv()

            @pl.when(position < n - 1)
            def _():
                red_send[k, at, :] = (base() + red_recv[k, at, :].astype(jnp.float32)).astype(jnp.bfloat16)
                red_copy(k, d, c).start()

            @pl.when(position == n - 1)
            def _():
                rebuilt = base() + red_recv[k, at, :].astype(jnp.float32)
                err[k, at, :] = (rebuilt - goal[k, at, :].astype(jnp.float32)).astype(jnp.bfloat16)
                hand_on(k, d, c)

    def gather_step(k, d, c):
        err_copy(k, d, c).wait_recv()
        hand_on(k, d, c)

    def on_chains(act, d, c):
        act(0, d, c)

        @pl.when(layer == last)
        def _():
            act(1, d, c)

    def chain(t, carry):
        for d in (0, 1):
            position = place(d)[0]
            c = t - position

            @pl.when((c >= 0) & (c < CHUNKS))
            def _():
                on_chains(reduce_step, d, c)

            g = t - (2 * (n - 1) - position)

            @pl.when((position < n - 1) & (g >= 0) & (g < CHUNKS))
            def _():
                on_chains(gather_step, d, g)

        return carry

    lax.fori_loop(0, CHUNKS + 2 * (n - 1), chain, 0)

    @pl.when(layer < last)
    def _():
        each_chunk(lambda d, c: next_copy(d, c).wait_recv())

    def grads_step(j, carry):
        at = aligned(j * ftile, ftile)
        grads = lax.dot_general(err[0], dec[0, at, :], NT, preferred_element_type=jnp.float32)
        grads = grads + lax.dot_general(err[1], dec[1, at, :], NT, preferred_element_type=jnp.float32)
        gated = jnp.where(codes[:, at].astype(jnp.float32) > 0, grads, 0.0)
        gsum[:, at] = gated.reshape(points, height, ftile).sum(axis=0).astype(jnp.bfloat16)
        return carry

    lax.fori_loop(0, ftiles, grads_step, 0)

    if scatter:
        block = width // groups

        def final_copy(sender, target):
            return pltpu.make_async_remote_copy(
                final_send.at[target], final_recv.at[sender], final_sem.at[0, target], final_sem.at[1, sender],
                device_id={"feat": target // paths, "path": lax.rem(target, paths)}, device_id_type=MESH,
            )

        def product(b):
            return lax.dot_general(gsum[...], enc[aligned(b * block, block), :], NT, preferred_element_type=jnp.float32)

        def send_block(i, carry):
            b = lax.rem(me + 1 + i, groups)
            final_send[b] = product(b).astype(jnp.bfloat16)
            final_copy(me, b).start()
            return carry

        lax.fori_loop(0, groups - 1, send_block, 0)
        part[...] = product(me)

        def take_block(i, carry):
            b = lax.rem(me + 1 + i, groups)
            final_copy(b, b).wait_recv()
            part[...] += final_recv[b].astype(jnp.float32)
            return carry

        lax.fori_loop(0, groups - 1, take_block, 0)
        offset_here = pick(pick_source, ctxb_ref) - pick(pick_donor, ctxb_ref)
        out_ref[...] = offset_here * part[...] / points

        def sent_block(i, carry):
            b = lax.rem(me + 1 + i, groups)
            final_copy(me, b).wait_send()
            return carry

        lax.fori_loop(0, groups - 1, sent_block, 0)
    else:
        out_ref[...] = lax.dot_general(gsum[...], enc[...], NT, preferred_element_type=jnp.float32)

    def sent(d, c):
        position = place(d)[0]

        def of_chain(k, d, c):
            @pl.when(position < n - 1)
            def _():
                red_copy(k, d, c).wait_send()

            @pl.when(position > 0)
            def _():
                err_copy(k, d, c).wait_send()

        @pl.when(layer < last)
        def _():
            later_copy(d, c).wait_send()

        on_chains(of_chain, d, c)

        @pl.when(layer > 0)
        def _():
            next_copy(d, c).wait_send()

    each_chunk(sent)


def per_device(shape, context, targets, beyond_targets, positions, donors, encoder, encoder_bias, decoder):
    layers, n, paths = shape
    path = lax.axis_index("path")
    height = positions.shape[0]
    width, feats = encoder.shape[1:]
    cols = decoder.shape[3]
    points = PTS_DEV * paths
    rows = points * height
    groups = n * paths
    block = width // groups
    me = lax.axis_index("feat") * paths + path
    scatter = block % 16 == 0
    ctx = context[0]
    tgt = lax.dynamic_slice_in_dim(targets[0], path * cols, cols, 1)
    bey = lax.dynamic_slice_in_dim(beyond_targets, path * cols, cols, 1)
    ctxb = lax.dynamic_slice_in_dim(ctx, me * block, block, 1)
    bf16, f32 = jnp.bfloat16, jnp.float32
    dma = pltpu.SemaphoreType.DMA
    final = (
        [
            pltpu.VMEM((height, block), f32),
            pltpu.VMEM((groups, height, block), bf16),
            pltpu.VMEM((groups, height, block), bf16),
        ]
        if scatter
        else [None, None, None]
    )
    scratch = [
        pltpu.VMEM((width, feats), bf16),
        pltpu.VMEM((2, feats, cols), bf16),
        pltpu.VMEM((rows, width), bf16),
        pltpu.VMEM((rows, feats), bf16),
        pltpu.VMEM((rows, cols), f32),
        pltpu.VMEM((rows, cols), bf16),
        pltpu.VMEM((rows, cols), bf16),
        pltpu.VMEM((2, rows, cols), bf16),
        pltpu.VMEM((2, rows, cols), bf16),
        pltpu.VMEM((2, rows, cols), bf16),
        pltpu.VMEM((2, rows, cols), bf16),
        pltpu.VMEM((height, feats), bf16),
        *final,
        dma((feats // tile_of(feats, 256),)),
        dma((2,)),
        dma((2, 2, CHUNKS)),
        dma((2, 2, 2, CHUNKS)),
        dma((2, 2, 2, CHUNKS)),
        dma((2, 2, CHUNKS)),
        dma((2, groups)) if scatter else None,
    ]
    kept = [s is not None for s in scratch]

    def body(*refs):
        fixed, given = refs[:10], iter(refs[10:])
        kernel(shape, *fixed, *[next(given) if k else None for k in kept])

    vmem, anywhere = pl.BlockSpec(memory_space=pltpu.VMEM), pl.BlockSpec(memory_space=pl.ANY)
    out = pl.pallas_call(
        body,
        out_shape=jax.ShapeDtypeStruct((height, block if scatter else width), f32),
        in_specs=[vmem] * 7 + [anywhere] * 2,
        out_specs=vmem,
        scratch_shapes=[s for s in scratch if s is not None],
        compiler_params=pltpu.CompilerParams(
            collective_id=0, has_side_effects=True, vmem_limit_bytes=60 * 1024 * 1024
        ),
        name="attribution",
    )(positions[:, None], donors[:, None], ctx, tgt, bey, encoder_bias, ctxb, encoder, decoder)
    if not scatter:
        quadrature = lax.psum_scatter(out, ("feat", "path"), scatter_dimension=1, tiled=True)
        offset = ctxb[positions].astype(f32) - ctxb[donors].astype(f32)
        out = offset * quadrature / points
    return out[None]


def solution(mesh):
    shape = tuple(mesh.shape[a] for a in ("layer", "feat", "path"))
    placed = (
        P("layer", None, None),
        P("layer", None, None),
        P(),
        P(),
        P(),
        P("layer", None, "feat"),
        P("layer", "feat"),
        P("layer", None, "feat", "path"),
    )
    return jax.shard_map(
        functools.partial(per_device, shape),
        mesh=mesh,
        in_specs=placed,
        out_specs=P("layer", None, ("feat", "path")),
        check_vma=False,
    )
```

time: 297 us -> 78 us (0.26)
  waiting for transfers between devices: 233 us -> 0 us
  Pallas kernels: 0 us -> 69.8 us
  matrix products: 27.3 us -> 0 us
  between operations: 13.3 us -> 0.01 us
  other arithmetic: 6.58 us -> 0 us
  starting transfers between devices: 6.12 us -> 0 us
    psum x1 -> x0, waiting for transfers between devices: 94.8 us -> none  [decode_errors(): own, later = lax.psum((parts[0], parts[1]), 'feat')]
    pallas_call x0 -> x1, Pallas kernels: none -> 69.8 us  [per_device(): pl.pallas_call(body, out_shape=jax.ShapeDtypeStruct((height, block if sca...]
    unnamed x5 -> x0, waiting for transfers between devices: 63.4 us -> none
    reduce_scatter x1 -> x0, waiting for transfers between devices: 29.5 us -> none  [per_device(): lax.psum_scatter(partial_grads, 'path', scatter_dimension=0, tiled=True)]
    dot_general x4 -> x0, matrix products: 27.3 us -> none  [the longest x1 7.84 us: per_device(): jnp.einsum('jrd,jfd->rf', errors, decoder[0], preferred_element_type=jnp....]
    all_gather x1 -> x0, waiting for transfers between devices: 23.3 us -> none  [per_device(): gathered = lax.all_gather(code_rows, 'path', axis=0, tiled=True)]
    ppermute x2 -> x0, waiting for transfers between devices: 22.4 us -> none  [from_behind(): return lax.ppermute(block, axis, route)]
    ppermute x2 -> x0, starting transfers between devices: 5.99 us -> none  [from_behind(): return lax.ppermute(block, axis, route)]
  transfers between devices with their start and end apart: 6 -> 0, of which waited for: 6 -> 0; matrix products, arithmetic and copies ran while one was open for 0% -> 0% of each run, Pallas kernels for 0% -> 0%
where the time goes in v1:
time: 78 us; the launch traced here: 77.7 us
  Pallas kernels  69.8 us (89%)
  local copies, waits for them, and re-layouts  7.91 us (10%)
    pallas_call x1, Pallas kernels, per_device(): pl.pallas_call(body, out_shape=jax.ShapeDtypeStruct((height, block if sca...  69.8 us
    dynamic_slice x1, local copies, waits for them, and re-layouts, per_device(): bey = lax.dynamic_slice_in_dim(beyond_targets, path * cols, cols, 1)  1.57 us

profile of v1, /device:TPU:1, one launch (start us, length us, event | category | flops | bytes accessed | tf_op | source)
XLA Modules:
  0.0 77.7 jit_solution(14290418148098733271)
XLA Ops:
  0.0 0.0 copy-start
  0.0 1.4 %copy.9.refs_0_ = s32[32,1]{1,0:T(8,128)} copy(s32[32,1]{0,1:T(1,128)} %bitcast.10) | data formatting | bytes 256 | tf_op jit(solution)/shard_map/broadcast_in_dim | solution.py:395
  1.4 1.3 %copy.10.refs_1_ = s32[32,1]{1,0:T(8,128)} copy(s32[32,1]{0,1:T(1,128)} %bitcast.11) | data formatting | bytes 256 | tf_op jit(solution)/shard_map/broadcast_in_dim | solution.py:395
  2.7 1.5 %dynamic-slice_bitcast_fusion.1.refs_6_ = bf16[64,288]{1,0:T(8,128)(2,1)} fusion(bf16[1,64,2304]{2,1,0:T(8,128)(2,1)} %param.8, s32[]{:T(128)S(6)} %select_n.8), kind=kLoop, calls=%fused_computation.1 | loop fusion | bytes 73732 | tf_op jit(solution)/shard_map/dynamic_slice | solution.py:344
  4.3 0.0 copy-done
  4.3 0.7 dynamic-slice_bitcast_fusion.refs_3_
  4.9 1.6 %constant_dynamic-slice_fusion.refs_4_ = bf16[64,1152]{1,0:T(8,128)(2,1)} fusion(bf16[64,2304]{1,0:T(8,128)(2,1)} %param.10, s32[]{:T(128)S(6)} %select_n.7), kind=kLoop, calls=%fused_computation.2 | loop fusion | bytes 294916 | tf_op jit(solution)/shard_map/dynamic_slice | solution.py:343
  6.5 69.8 %attribution.1 = f32[32,288]{1,0:T(8,128)} custom-call(s32[32,1]{1,0:T(8,128)} %copy.9.refs_0_, s32[32,1]{1,0:T(8,128)} %copy.10.refs_1_, bf16[64,2304]{1,0:T(8,128)(2,1)} %bitcast.8, bf16[64,1152]{1,0:T(8,128)(2,1)} %dynamic-slice_bitcast_fusion.refs_3_, bf16[64,1152]{1,0:T(8,128)(2,1)} %constant_dynamic-slice_fusion.refs_4_, f32[1,2048]{1,0:T(1,128)} %refs_5_.1, ...), custom_call_target="tpu_custom_call" | custom-call | tf_op jit(solution)/shard_map/attribution/pallas_call | solution.py:385
  76.3 1.4 %copy.12 = f32[1,32,288]{2,1,0:T(8,128)} copy(f32[1,32,288]{2,1,0:T(8,128)} %bitcast.9) | data formatting | bytes 73728
Async XLA Ops:
  0.0 4.3 %copy-start = (bf16[1,64,2304]{2,1,0:T(8,128)(2,1)S(1)}, bf16[1,64,2304]{2,1,0:T(8,128)(2,1)}, u32[]{:S(2)}) copy-start(bf16[1,64,2304]{2,1,0:T(8,128)(2,1)} %param.9) | copy-start | bytes 884740

commit v2 on v1

--- a/solution.py
+++ b/solution.py
@@ -9,6 +9,7 @@
 
 PTS_DEV = 4
 CHUNKS = 8
+SKEW = 4
 MESH = pl.DeviceIdType.MESH
 NT = (((1,), (1,)), ((), ()))
 
@@ -23,14 +24,14 @@
 
 
 def kernel(
-    shape, pos_ref, don_ref, ctx_ref, tgt_ref, bey_ref, bias_ref, ctxb_ref, enc_hbm, dec_hbm, out_ref,
-    enc, dec, inputs, codes, own, later, later_in, goal, red_recv, red_send, err, gsum, part, final_send, final_recv,
+    shape, pos_ref, don_ref, ctx_ref, tgt_ref, bey_ref, bias_ref, enc_hbm, dec_hbm, out_ref,
+    enc, dec, inputs, codes, own, later, later_in, goal, red_recv, red_send, err, gsum, part, offsets, final_send, final_recv,
     enc_sem, dec_sem, later_sem, red_sem, err_sem, next_sem, final_sem,
 ):
     layers, n, paths = shape
     layer, z, path = lax.axis_index("layer"), lax.axis_index("feat"), lax.axis_index("path")
     last = layers - 1
-    height, tokens = pos_ref.shape[0], ctx_ref.shape[0]
+    height, tokens = pos_ref.shape[1], ctx_ref.shape[1]
     rows, width = inputs.shape
     feats, cols = codes.shape[1], own.shape[1]
     points = rows // height
@@ -75,22 +76,17 @@
     dec_copy(1).start()
     dec_copy(0).start()
 
-    token = lax.broadcasted_iota(jnp.int32, (height, tokens), 1)
-    pick_source = (token == pos_ref[...]).astype(jnp.float32).astype(jnp.bfloat16)
-    pick_donor = (token == don_ref[...]).astype(jnp.float32).astype(jnp.bfloat16)
-
-    def pick(which, ref):
-        return jnp.dot(which, ref[...], preferred_element_type=jnp.float32)
-
-    donor = pick(pick_donor, ctx_ref)
-    offset = pick(pick_source, ctx_ref) - donor
+    token = lax.broadcasted_iota(jnp.int32, (tokens, height), 0)
+    pick_source = (token == pos_ref[...]).astype(jnp.float32).T.astype(jnp.bfloat16)
+    pick_donor = (token == don_ref[...]).astype(jnp.float32).T.astype(jnp.bfloat16)
+
+    def pick(which, table):
+        return jnp.dot(which, table, preferred_element_type=jnp.float32)
+
+    donor = pick(pick_donor, ctx_ref[0])
+    offset = pick(pick_source, ctx_ref[0]) - donor
     for p in range(points):
         inputs[p * height : (p + 1) * height, :] = (donor + ((p + 0.5) / points) * offset).astype(jnp.bfloat16)
-    goals = (pick(pick_source, tgt_ref).astype(jnp.bfloat16), pick(pick_source, bey_ref).astype(jnp.bfloat16))
-    for p in range(points):
-        for k in (0, 1):
-            goal[k, p * height : (p + 1) * height, :] = goals[k]
-
     @pl.when(layer == 0)
     def _():
         later_in[...] = jnp.zeros_like(later_in)
@@ -171,6 +167,19 @@
 
     decode(0, own)
 
+    if tgt_ref.shape[2] == cols:
+        goal_at = slice(None)
+    else:
+        goal_at = aligned(path * cols, cols)
+    goals = [pick(pick_source, table).astype(jnp.bfloat16) for table in (tgt_ref[0, :, goal_at], bey_ref[:, goal_at])]
+    for p in range(points):
+        for k in (0, 1):
+            goal[k, p * height : (p + 1) * height, :] = goals[k]
+    if scatter:
+        block = width // groups
+        for b in range(groups):
+            offsets[b] = offset[:, b * block : (b + 1) * block]
+
     def hand_on(k, d, c):
         @pl.when(place(d)[0] > 0)
         def _():
@@ -231,13 +240,13 @@
     def chain(t, carry):
         for d in (0, 1):
             position = place(d)[0]
-            c = t - position
+            c = t - SKEW * position
 
             @pl.when((c >= 0) & (c < CHUNKS))
             def _():
                 on_chains(reduce_step, d, c)
 
-            g = t - (2 * (n - 1) - position)
+            g = t - SKEW * (2 * (n - 1) - position)
 
             @pl.when((position < n - 1) & (g >= 0) & (g < CHUNKS))
             def _():
@@ -245,7 +254,7 @@
 
         return carry
 
-    lax.fori_loop(0, CHUNKS + 2 * (n - 1), chain, 0)
+    lax.fori_loop(0, CHUNKS + SKEW * 2 * (n - 1), chain, 0)
 
     @pl.when(layer < last)
     def _():
@@ -262,7 +271,6 @@
     lax.fori_loop(0, ftiles, grads_step, 0)
 
     if scatter:
-        block = width // groups
 
         def final_copy(sender, target):
             return pltpu.make_async_remote_copy(
@@ -289,8 +297,7 @@
             return carry
 
         lax.fori_loop(0, groups - 1, take_block, 0)
-        offset_here = pick(pick_source, ctxb_ref) - pick(pick_donor, ctxb_ref)
-        out_ref[...] = offset_here * part[...] / points
+        out_ref[...] = offsets[me] * part[...] / points
 
         def sent_block(i, carry):
             b = lax.rem(me + 1 + i, groups)
@@ -338,20 +345,20 @@
     block = width // groups
     me = lax.axis_index("feat") * paths + path
     scatter = block % 16 == 0
-    ctx = context[0]
-    tgt = lax.dynamic_slice_in_dim(targets[0], path * cols, cols, 1)
-    bey = lax.dynamic_slice_in_dim(beyond_targets, path * cols, cols, 1)
-    ctxb = lax.dynamic_slice_in_dim(ctx, me * block, block, 1)
+    if cols % 128:
+        targets = lax.dynamic_slice_in_dim(targets, path * cols, cols, 2)
+        beyond_targets = lax.dynamic_slice_in_dim(beyond_targets, path * cols, cols, 1)
     bf16, f32 = jnp.bfloat16, jnp.float32
     dma = pltpu.SemaphoreType.DMA
     final = (
         [
             pltpu.VMEM((height, block), f32),
+            pltpu.VMEM((groups, height, block), f32),
             pltpu.VMEM((groups, height, block), bf16),
             pltpu.VMEM((groups, height, block), bf16),
         ]
         if scatter
-        else [None, None, None]
+        else [None, None, None, None]
     )
     scratch = [
         pltpu.VMEM((width, feats), bf16),
@@ -378,23 +385,24 @@
     kept = [s is not None for s in scratch]
 
     def body(*refs):
-        fixed, given = refs[:10], iter(refs[10:])
+        fixed, given = refs[:9], iter(refs[9:])
         kernel(shape, *fixed, *[next(given) if k else None for k in kept])
 
     vmem, anywhere = pl.BlockSpec(memory_space=pltpu.VMEM), pl.BlockSpec(memory_space=pl.ANY)
     out = pl.pallas_call(
         body,
         out_shape=jax.ShapeDtypeStruct((height, block if scatter else width), f32),
-        in_specs=[vmem] * 7 + [anywhere] * 2,
+        in_specs=[vmem] * 6 + [anywhere] * 2,
         out_specs=vmem,
         scratch_shapes=[s for s in scratch if s is not None],
         compiler_params=pltpu.CompilerParams(
             collective_id=0, has_side_effects=True, vmem_limit_bytes=60 * 1024 * 1024
         ),
         name="attribution",
-    )(positions[:, None], donors[:, None], ctx, tgt, bey, encoder_bias, ctxb, encoder, decoder)
+    )(positions[None], donors[None], context, targets, beyond_targets, encoder_bias, encoder, decoder)
     if not scatter:
         quadrature = lax.psum_scatter(out, ("feat", "path"), scatter_dimension=1, tiled=True)
+        ctxb = lax.dynamic_slice_in_dim(context[0], me * block, block, 1)
         offset = ctxb[positions].astype(f32) - ctxb[donors].astype(f32)
         out = offset * quadrature / points
     return out[None]

time: 78 us -> 57.8 us (0.74)
  Pallas kernels: 69.8 us -> 56.2 us
  local copies, waits for them, and re-layouts: 7.91 us -> 1.42 us
    pallas_call x1, Pallas kernels: 69.8 us -> 56.2 us  [per_device(): pl.pallas_call(body, out_shape=jax.ShapeDtypeStruct((height, block if sca...]
    dynamic_slice x3 -> x0, local copies, waits for them, and re-layouts: 3.77 us -> none  [the longest x1 1.57 us: per_device(): bey = lax.dynamic_slice_in_dim(beyond_targets, path * cols, cols, 1)]
    broadcast_in_dim x2 -> x0, local copies, waits for them, and re-layouts: 2.72 us -> none  [the longest x1 1.38 us: per_device(): positions[:, None]]
where the time goes in v2:
time: 57.8 us; the launch traced here: 57.6 us
  Pallas kernels  56.2 us (97%)
  local copies, waits for them, and re-layouts  1.42 us (2%)
    pallas_call x1, Pallas kernels, per_device(): pl.pallas_call(body, out_shape=jax.ShapeDtypeStruct((height, block if sca...  56.2 us
    unnamed x1, local copies, waits for them, and re-layouts  1.42 us

profile of v2, /device:TPU:1, one launch (start us, length us, event | category | flops | bytes accessed | tf_op | source)
XLA Modules:
  0.0 57.6 jit_solution(5372692393158083434)
XLA Ops:
  0.0 56.2 %attribution.1 = f32[32,288]{1,0:T(8,128)} custom-call(s32[1,32]{1,0:T(1,128)} %bitcast.4, s32[1,32]{1,0:T(1,128)} %bitcast.5, bf16[1,64,2304]{2,1,0:T(8,128)(2,1)} %refs_2_.1, bf16[1,64,2304]{2,1,0:T(8,128)(2,1)} %refs_3_.1, bf16[64,2304]{1,0:T(8,128)(2,1)} %refs_4_.1, f32[1,2048]{1,0:T(1,128)} %refs_5_.1, bf16[1,2304,2048]{2,1,0:T(8,128)(2,1)} %refs_6_.1, ...), custom_call_target="tpu_custom_call" | custom-call | tf_op jit(solution)/shard_map/attribution/pallas_call | solution.py:392
  56.2 1.4 %copy.10 = f32[1,32,288]{2,1,0:T(8,128)} copy(f32[1,32,288]{2,1,0:T(8,128)} %bitcast.3) | data formatting | bytes 73728

commit v3 on v2

--- a/solution.py
+++ b/solution.py
@@ -8,8 +8,9 @@
 from jax.sharding import PartitionSpec as P
 
 PTS_DEV = 4
-CHUNKS = 8
-SKEW = 4
+CHUNKS = 4
+SKEW = 6
+LEAD = 4
 MESH = pl.DeviceIdType.MESH
 NT = (((1,), (1,)), ((), ()))
 
@@ -36,7 +37,10 @@
     feats, cols = codes.shape[1], own.shape[1]
     points = rows // height
     half = rows // 2
+    ctile = tile_of(cols, 384)
+    ctiles = cols // ctile
     chunk = half // CHUNKS
+    chunks = CHUNKS * ctiles
     groups = n * paths
     me = z * paths + path
     scatter = final_send is not None
@@ -73,8 +77,6 @@
 
     for j in range(ftiles):
         enc_copy(j).start()
-    dec_copy(1).start()
-    dec_copy(0).start()
 
     token = lax.broadcasted_iota(jnp.int32, (tokens, height), 0)
     pick_source = (token == pos_ref[...]).astype(jnp.float32).T.astype(jnp.bfloat16)
@@ -93,6 +95,12 @@
 
     def encode(j, carry):
         enc_copy(j).wait()
+        for k in (0, 1):
+
+            @pl.when(j == max(ftiles - LEAD - k, 0))
+            def _():
+                dec_copy(k).start()
+
         at = aligned(j * ftile, ftile)
         preact = jnp.dot(inputs[...], enc[:, at], preferred_element_type=jnp.float32) + bias_ref[:, at]
         codes[:, at] = jnp.maximum(preact, 0.0).astype(jnp.bfloat16)
@@ -100,29 +108,24 @@
 
     lax.fori_loop(0, ftiles, encode, 0)
 
-    ctile = tile_of(cols, 384)
-
-    def decode(k, into):
-        def step(j, carry):
-            at = aligned(j * ctile, ctile) if cols > ctile else slice(None)
-            value = jnp.dot(codes[...], dec[k, :, at], preferred_element_type=jnp.float32)
-            into[:, at] = value.astype(into.dtype)
-            return carry
-
-        dec_copy(k).wait()
-        lax.fori_loop(0, cols // ctile, step, 0)
-
-    decode(1, later)
-
+    def columns(j):
+        return aligned(j * ctile, ctile) if ctiles > 1 else slice(None)
+
+    def decode(k, into, j):
+        at = columns(j)
+        value = jnp.dot(codes[...], dec[k, :, at], preferred_element_type=jnp.float32)
+        into[:, at] = value.astype(into.dtype)
+
+    dec_copy(1).wait()
     pl.semaphore_wait(barrier, groups - 1 + jnp.minimum(layer, 1) + jnp.minimum(last - layer, 1))
 
     def at_rows(d, c):
-        return aligned(d * half + c * chunk, chunk)
+        return aligned(d * half + lax.rem(c, CHUNKS) * chunk, chunk), columns(c // CHUNKS)
 
     def later_copy(d, c):
         at = at_rows(d, c)
         return pltpu.make_async_remote_copy(
-            later.at[at, :], later_in.at[at, :], later_sem.at[0, d, c], later_sem.at[1, d, c],
+            later.at[*at], later_in.at[*at], later_sem.at[0, d, c], later_sem.at[1, d, c],
             device_id={"layer": lax.rem(layer + 1, layers)}, device_id_type=MESH,
         )
 
@@ -135,21 +138,21 @@
     def red_copy(k, d, c):
         at = at_rows(d, c)
         return pltpu.make_async_remote_copy(
-            red_send.at[k, at, :], red_recv.at[k, at, :], red_sem.at[0, k, d, c], red_sem.at[1, k, d, c],
+            red_send.at[k, *at], red_recv.at[k, *at], red_sem.at[0, k, d, c], red_sem.at[1, k, d, c],
             device_id={"feat": wrap(place(d)[1])}, device_id_type=MESH,
         )
 
     def err_copy(k, d, c):
         at = at_rows(d, c)
         return pltpu.make_async_remote_copy(
-            err.at[k, at, :], err.at[k, at, :], err_sem.at[0, k, d, c], err_sem.at[1, k, d, c],
+            err.at[k, *at], err.at[k, *at], err_sem.at[0, k, d, c], err_sem.at[1, k, d, c],
             device_id={"feat": wrap(place(d)[2])}, device_id_type=MESH,
         )
 
     def next_copy(d, c):
         at = at_rows(d, c)
         return pltpu.make_async_remote_copy(
-            err.at[0, at, :], err.at[1, at, :], next_sem.at[0, d, c], next_sem.at[1, d, c],
+            err.at[0, *at], err.at[1, *at], next_sem.at[0, d, c], next_sem.at[1, d, c],
             device_id={"layer": lax.rem(layer + last, layers)}, device_id_type=MESH,
         )
 
@@ -159,22 +162,18 @@
                 act(d, c)
             return carry
 
-        lax.fori_loop(0, CHUNKS, step, 0)
-
-    @pl.when(layer < last)
-    def _():
-        each_chunk(lambda d, c: later_copy(d, c).start())
-
-    decode(0, own)
-
-    if tgt_ref.shape[2] == cols:
-        goal_at = slice(None)
-    else:
-        goal_at = aligned(path * cols, cols)
-    goals = [pick(pick_source, table).astype(jnp.bfloat16) for table in (tgt_ref[0, :, goal_at], bey_ref[:, goal_at])]
-    for p in range(points):
-        for k in (0, 1):
-            goal[k, p * height : (p + 1) * height, :] = goals[k]
+        lax.fori_loop(0, chunks, step, 0)
+
+    def fill_goals():
+        if tgt_ref.shape[2] == cols:
+            goal_at = slice(None)
+        else:
+            goal_at = aligned(path * cols, cols)
+        goals = [pick(pick_source, table).astype(jnp.bfloat16) for table in (tgt_ref[0, :, goal_at], bey_ref[:, goal_at])]
+        for p in range(points):
+            for k in (0, 1):
+                goal[k, p * height : (p + 1) * height, :] = goals[k]
+
     if scatter:
         block = width // groups
         for b in range(groups):
@@ -197,8 +196,8 @@
 
         def base():
             if k == 1:
-                return later[at, :].astype(jnp.float32)
-            return own[at, :] + later_in[at, :].astype(jnp.float32)
+                return later[*at].astype(jnp.float32)
+            return own[*at] + later_in[*at].astype(jnp.float32)
 
         if k == 0:
 
@@ -208,7 +207,7 @@
 
         @pl.when(position == 0)
         def _():
-            red_send[k, at, :] = base().astype(jnp.bfloat16)
+            red_send[k, *at] = base().astype(jnp.bfloat16)
             red_copy(k, d, c).start()
 
         @pl.when(position > 0)
@@ -217,13 +216,13 @@
 
             @pl.when(position < n - 1)
             def _():
-                red_send[k, at, :] = (base() + red_recv[k, at, :].astype(jnp.float32)).astype(jnp.bfloat16)
+                red_send[k, *at] = (base() + red_recv[k, *at].astype(jnp.float32)).astype(jnp.bfloat16)
                 red_copy(k, d, c).start()
 
             @pl.when(position == n - 1)
             def _():
-                rebuilt = base() + red_recv[k, at, :].astype(jnp.float32)
-                err[k, at, :] = (rebuilt - goal[k, at, :].astype(jnp.float32)).astype(jnp.bfloat16)
+                rebuilt = base() + red_recv[k, *at].astype(jnp.float32)
+                err[k, *at] = (rebuilt - goal[k, *at].astype(jnp.float32)).astype(jnp.bfloat16)
                 hand_on(k, d, c)
 
     def gather_step(k, d, c):
@@ -242,19 +241,44 @@
             position = place(d)[0]
             c = t - SKEW * position
 
-            @pl.when((c >= 0) & (c < CHUNKS))
+            @pl.when((c >= 0) & (c < chunks))
             def _():
                 on_chains(reduce_step, d, c)
 
             g = t - SKEW * (2 * (n - 1) - position)
 
-            @pl.when((position < n - 1) & (g >= 0) & (g < CHUNKS))
+            @pl.when((position < n - 1) & (g >= 0) & (g < chunks))
             def _():
                 on_chains(gather_step, d, g)
 
         return carry
 
-    lax.fori_loop(0, CHUNKS + SKEW * 2 * (n - 1), chain, 0)
+    def later_tile(j, carry):
+        decode(1, later, j)
+
+        @pl.when(layer < last)
+        def _():
+            for i in range(CHUNKS):
+                for d in (0, 1):
+                    later_copy(d, j * CHUNKS + i).start()
+
+        return carry
+
+    def own_tile(j, carry):
+        decode(0, own, j)
+        lax.fori_loop(j * CHUNKS, (j + 1) * CHUNKS, chain, 0)
+        return carry
+
+    lax.fori_loop(0, ctiles, later_tile, 0)
+    dec_copy(0).wait()
+
+    goals_late = SKEW * (n - 1) >= chunks
+    if not goals_late:
+        fill_goals()
+    lax.fori_loop(0, ctiles, own_tile, 0)
+    if goals_late:
+        fill_goals()
+    lax.fori_loop(chunks, chunks + SKEW * 2 * (n - 1), chain, 0)
 
     @pl.when(layer < last)
     def _():
@@ -282,13 +306,21 @@
             return lax.dot_general(gsum[...], enc[aligned(b * block, block), :], NT, preferred_element_type=jnp.float32)
 
         def send_block(i, carry):
-            b = lax.rem(me + 1 + i, groups)
-            final_send[b] = product(b).astype(jnp.bfloat16)
-            final_copy(me, b).start()
+            row = i // paths
+            b = jnp.where(2 * z < n, n - 1 - row, row) * paths + lax.rem(path + 1 + i, paths)
+
+            @pl.when(b == me)
+            def _():
+                part[...] = product(b)
+
+            @pl.when(b != me)
+            def _():
+                final_send[b] = product(b).astype(jnp.bfloat16)
+                final_copy(me, b).start()
+
             return carry
 
-        lax.fori_loop(0, groups - 1, send_block, 0)
-        part[...] = product(me)
+        lax.fori_loop(0, groups, send_block, 0)
 
         def take_block(i, carry):
             b = lax.rem(me + 1 + i, groups)
@@ -350,6 +382,7 @@
         beyond_targets = lax.dynamic_slice_in_dim(beyond_targets, path * cols, cols, 1)
     bf16, f32 = jnp.bfloat16, jnp.float32
     dma = pltpu.SemaphoreType.DMA
+    chunks = CHUNKS * (cols // tile_of(cols, 384))
     final = (
         [
             pltpu.VMEM((height, block), f32),
@@ -376,10 +409,10 @@
         *final,
         dma((feats // tile_of(feats, 256),)),
         dma((2,)),
-        dma((2, 2, CHUNKS)),
-        dma((2, 2, 2, CHUNKS)),
-        dma((2, 2, 2, CHUNKS)),
-        dma((2, 2, CHUNKS)),
+        dma((2, 2, chunks)),
+        dma((2, 2, 2, chunks)),
+        dma((2, 2, 2, chunks)),
+        dma((2, 2, chunks)),
         dma((2, groups)) if scatter else None,
     ]
     kept = [s is not None for s in scratch]

time: 57.8 us -> 56.2 us (0.972)
  Pallas kernels: 56.2 us -> 54.5 us
    pallas_call x1, Pallas kernels: 56.2 us -> 54.5 us  [per_device(): pl.pallas_call(body, out_shape=jax.ShapeDtypeStruct((height, block if sca...]
where the time goes in v3:
time: 56.2 us; the launch traced here: 56 us
  Pallas kernels  54.5 us (97%)
  local copies, waits for them, and re-layouts  1.42 us (3%)
    pallas_call x1, Pallas kernels, per_device(): pl.pallas_call(body, out_shape=jax.ShapeDtypeStruct((height, block if sca...  54.5 us
    unnamed x1, local copies, waits for them, and re-layouts  1.42 us

profile of v3, /device:TPU:1, one launch (start us, length us, event | category | flops | bytes accessed | tf_op | source)
XLA Modules:
  0.0 56.0 jit_solution(13569432709106825519)
XLA Ops:
  0.0 54.5 %attribution.1 = f32[32,288]{1,0:T(8,128)} custom-call(s32[1,32]{1,0:T(1,128)} %bitcast.4, s32[1,32]{1,0:T(1,128)} %bitcast.5, bf16[1,64,2304]{2,1,0:T(8,128)(2,1)} %refs_2_.1, bf16[1,64,2304]{2,1,0:T(8,128)(2,1)} %refs_3_.1, bf16[64,2304]{1,0:T(8,128)(2,1)} %refs_4_.1, f32[1,2048]{1,0:T(1,128)} %refs_5_.1, bf16[1,2304,2048]{2,1,0:T(8,128)(2,1)} %refs_6_.1, ...), custom_call_target="tpu_custom_call" | custom-call | tf_op jit(solution)/shard_map/attribution/pallas_call | solution.py:425
  54.5 1.4 %copy.10 = f32[1,32,288]{2,1,0:T(8,128)} copy(f32[1,32,288]{2,1,0:T(8,128)} %bitcast.3) | data formatting | bytes 73728
